TPU v7x, 256 devices: a whole 4x4x8 slice. The times are simulated.
256 devices in a mesh: wide: 32 (over x, y, core), narrow: 8 (over z).
Axes of the slice: x: 4, y: 4, z: 8, core: 2. Of those that a mesh axis runs over, the one named last changes fastest.
Arguments:
- blocks: bfloat16 [32, 8, 16, 64, 4096], P('wide', 'narrow'), may hold values from -16 to 16
- row_tile: int32 [32, 8, 16], P('wide', 'narrow'), may hold values from 0 to 15
- col_tile: int32 [32, 8, 16], P('wide', 'narrow'), may hold values from 0 to 63, as said below
- depth_tile: int32 [32, 8, 16], P('wide', 'narrow'), may hold values from 0 to 15
- block_count: int32 [32, 8], P('wide', 'narrow'), may hold values from 4 to 16, as said below
- factor_b: bfloat16 [32768, 256], P(('wide', 'narrow')), may hold values from -40 to 40
- factor_c: bfloat16 [1024, 256], replicated, may hold values from -0.076293945 to 0.076293945
Outputs:
- a_new: float32 [32768, 256], P(('wide', 'narrow'))
- b_new: float32 [32768, 256], P(('wide', 'narrow'))
Inputs may be any that keep to these rules, and one draw needn't show every extreme that they name: `block_count`: every device holds at least 4 live blocks, and some device exactly 16. col_tile // 2 is the index of wide that holds the block's mode-2 factor rows; among the 16 slots of one device, live or not, each such index appears at most 1 times, and some index exactly 1 times.
All inputs are finite; a program needn't handle non-finite values.
Results may differ from a plain program's by a relative error of at most 0.02.
Values may be sent and summed in bfloat16 or wider, within the bound.
No kernel may reach another device: no remote copies, remote signals or barrier semaphores. Data moves between devices by JAX's collectives and lax.ppermute only.
A program may use at most 128 MiB of HBM per device.

v0:
```python
import jax
import jax.numpy as jnp
from jax import lax
from jax.sharding import PartitionSpec as P

TI_DEV = 2


def right_solve(target, matrix):
    chol_lower = jnp.linalg.cholesky(matrix)
    middle = lax.linalg.triangular_solve(
        chol_lower, target, left_side=False, lower=True, transpose_a=True
    )
    return lax.linalg.triangular_solve(
        chol_lower, middle, left_side=False, lower=True, transpose_a=False
    )


def column_gram(matrix):
    return lax.dot_general(
        matrix, matrix, (((0,), (0,)), ((), ())), preferred_element_type=jnp.float32
    )


def depth_mix(one_block, depth_id, factor_c, tile_rows):
    depth_rows = lax.dynamic_slice_in_dim(factor_c, depth_id * tile_rows, tile_rows, 0)
    depth_mixed = lax.dot_general(
        one_block, depth_rows, (((0,), (0,)), ((), ())), preferred_element_type=jnp.float32
    )
    return depth_mixed.reshape(tile_rows, tile_rows, depth_rows.shape[1])


def local(blocks, row_tile, col_tile, depth_tile, block_count, factor_b, factor_c):
    local_blocks = blocks[0, 0]
    first_ids = row_tile[0, 0]
    second_ids = col_tile[0, 0]
    depth_ids = depth_tile[0, 0]
    live_count = block_count[0, 0]
    tile_rows = local_blocks.shape[1]
    rank_width = factor_c.shape[1]
    wide_count = lax.axis_size("wide")
    narrow_count = lax.axis_size("narrow")
    second_local = factor_b.shape[0] // tile_rows
    owners = second_ids // second_local
    inside = second_ids % second_local
    gram_c = column_gram(factor_c)
    gram_b = lax.psum(column_gram(factor_b), ("wide", "narrow"))
    gathered = lax.all_gather(factor_b, "wide", axis=0, tiled=True)
    b_tiles = gathered.reshape(wide_count * second_local, tile_rows, rank_width)
    b_pick = owners * second_local + inside

    def first_step(slot_index, partial_sum):
        one_block = lax.dynamic_index_in_dim(local_blocks, slot_index, 0, False)
        depth_mixed = depth_mix(one_block, depth_ids[slot_index], factor_c, tile_rows)
        b_rows = lax.dynamic_index_in_dim(b_tiles, b_pick[slot_index], 0, False).astype(jnp.float32)
        b_term = jnp.sum(depth_mixed * b_rows[None, :, :], axis=1)
        target = first_ids[slot_index]
        current = lax.dynamic_index_in_dim(partial_sum, target, 0, False)
        return lax.dynamic_update_index_in_dim(partial_sum, current + b_term, target, 0)

    first_part = lax.fori_loop(
        0,
        live_count,
        first_step,
        jnp.zeros((narrow_count * TI_DEV, tile_rows, rank_width), jnp.float32),
    )
    mttkrp_a = lax.psum_scatter(
        first_part.reshape(-1, rank_width), "narrow", scatter_dimension=0, tiled=True
    )
    a_new = right_solve(mttkrp_a, gram_b * gram_c)
    a_half = a_new.astype(jnp.bfloat16)
    a_rows = lax.all_gather(a_half, "narrow", axis=0, tiled=True)
    gram_a = lax.psum(column_gram(a_half), ("wide", "narrow"))
    a_tiles = a_rows.reshape(a_rows.shape[0] // tile_rows, tile_rows, rank_width)
    width_slots = wide_count * second_local
    second_pick = owners * second_local + inside

    def second_step(slot_index, partial_sum):
        one_block = lax.dynamic_index_in_dim(local_blocks, slot_index, 0, False)
        depth_mixed = depth_mix(one_block, depth_ids[slot_index], factor_c, tile_rows)
        a_part = lax.dynamic_index_in_dim(a_tiles, first_ids[slot_index], 0, False).astype(
            jnp.float32
        )
        a_term = jnp.sum(depth_mixed * a_part[:, None, :], axis=0)
        target = second_pick[slot_index]
        current = lax.dynamic_index_in_dim(partial_sum, target, 0, False)
        return lax.dynamic_update_index_in_dim(partial_sum, current + a_term, target, 0)

    second_part = lax.fori_loop(
        0, live_count, second_step, jnp.zeros((width_slots, tile_rows, rank_width), jnp.float32)
    )
    mttkrp_b = lax.psum_scatter(
        second_part.reshape(-1, rank_width), "wide", scatter_dimension=0, tiled=True
    )
    b_new = right_solve(mttkrp_b, gram_a * gram_c)
    return (a_new, b_new)


def solution(mesh):
    return jax.shard_map(
        local,
        mesh=mesh,
        in_specs=(
            P("wide", "narrow", None, None, None),
            P("wide", "narrow", None),
            P("wide", "narrow", None),
            P("wide", "narrow", None),
            P("wide", "narrow"),
            P(("wide", "narrow"), None),
            P(),
        ),
        out_specs=(P(("wide", "narrow"), None), P(("wide", "narrow"), None)),
        check_vma=False,
    )
```

profile of v0, /device:TPU:2, one launch (start us, length us, event | category | flops | bytes accessed | tf_op | source)
XLA Modules:
  0.0 688.1 jit_solution(2137662635349681206)
XLA Ops:
  8.8 1.8 fusion.35
  10.8 15.6 %copy.22 = bf16[1,1,16,64,4096]{3,4,2,1,0:T(8,128)(2,1)} copy(bf16[1,1,16,64,4096]{4,3,2,1,0:T(8,128)(2,1)} %param.16) | data formatting | bytes 16777216 | tf_op args[0]
  26.4 36.2 %all-gather.2.cloned.1.call-done = bf16[4096,256]{1,0:T(8,128)(2,1)} async-done(((bf16[128,256]{1,0:T(8,128)(2,1)}), bf16[4096,256]{1,0:T(8,128)(2,1)}) %all-gather.2.cloned.1.call-update) | async-done | bytes 2097168 | tf_op jit(solution)/shard_map/all_gather | solution.py:48
  62.7 144.2 %while.28 = (s32[]{:T(128)}, f32[16,64,256]{2,1,0:T(8,128)S(1)}, s32[]{:T(128)}, s32[16]{0:T(128)S(1)}, bf16[16,64,4096]{1,2,0:T(8,128)(2,1)}, /*index=5*/s32[16...) while((s32[]{:T(128)}, f32[16,64,256]{2,1,0:T(8,128)S(1)}, ...), condition=%wide.region_7.9_spmd, body=%wide.region_5.8_spmd.sunk | while | flops 136331280 | bytes 2556253 | solution.py:61
  207.9 64.7 %all-reduce.4.cloned.1.call-done = f32[256,256]{0,1:T(8,128)} async-done(((f32[256,256]{0,1:T(8,128)}), f32[256,256]{0,1:T(8,128)}) %all-reduce.4.cloned.1.call-update) | async-done | bytes 262160 | tf_op jit(solution)/shard_map/psum | solution.py:47
  274.1 11.7 %cholesky.130 = f32[128,128]{1,0:T(8,128)S(1)} custom-call(f32[128,128]{1,0:T(8,128)S(1)} %cholesky.194), custom_call_target="Cholesky" | custom-call | tf_op jit(solution)/shard_map/jit(cholesky)/cholesky | solution.py:10
  285.9 9.8 %custom-call.17 = f32[1,128,128]{1,2,0:T(8,128)S(1)} custom-call(f32[1,128,128]{2,1,0:T(8,128)S(1)} %get-tuple-element.211), custom_call_target="InvertDiagBlocksLowerTriangular" | custom-call | tf_op jit(solution)/shard_map/jit(cholesky)/cholesky | solution.py:10
  296.2 11.7 %cholesky.147 = f32[128,128]{1,0:T(8,128)S(1)} custom-call(f32[128,128]{1,0:T(8,128)S(1)} %convolution_subtract_fusion.5), custom_call_target="Cholesky" | custom-call | tf_op jit(solution)/shard_map/jit(cholesky)/cholesky | solution.py:10
  310.0 4.2 while.30
  314.2 19.7 %custom-call.18 = f32[2,128,128]{1,2,0:T(8,128)S(1)} custom-call(f32[2,128,128]{2,1,0:T(8,128)S(1)} %get-tuple-element.131), custom_call_target="InvertDiagBlocksLowerTriangular" | custom-call | tf_op jit(solution)/shard_map/triangular_solve/custom-call.0 | solution.py:11
  337.2 24.6 %all_gather.7 = bf16[1024,256]{0,1:T(8,128)(2,1)S(1)} all-gather(bf16[128,256]{0,1:T(8,128)(2,1)S(1)} %fusion.31), channel_id=1, replica_groups=mesh['wide'=32,'narrow'=8] {'narrow'}, dimensions={0}, use_global_device_ids=true | all-gather | bytes 589824 | tf_op jit(solution)/shard_map/all_gather | solution.py:72
  362.9 2.4 broadcast_in_dim.14
  365.4 159.6 %while.29 = (s32[]{:T(128)}, f32[64,64,256]{2,1,0:T(8,128)}, s32[]{:T(128)}, s32[16]{0:T(128)S(1)}, bf16[16,64,4096]{1,2,0:T(8,128)(2,1)}, /*index=5*/s32[16]{0:...) while((s32[]{:T(128)}, f32[64,64,256]{2,1,0:T(8,128)}, ...), condition=%wide.region_12.16_spmd, body=%wide.region_10.15_spmd.sunk | while | flops 136331280 | bytes 2556253 | solution.py:89
  374.5 1.5 fusion.72
  385.1 1.5 fusion.72
  395.7 1.5 fusion.72
  406.3 1.5 fusion.72
  416.9 1.5 fusion.72
  427.5 1.5 fusion.72
  448.6 1.5 fusion.72
  459.2 1.5 fusion.72
  469.8 1.5 fusion.72
  480.4 1.5 fusion.72
  491.0 1.5 fusion.72
  512.2 1.5 fusion.72
  522.8 1.5 fusion.72
  525.7 89.8 %all-reduce.6.cloned.1.call-done = f32[256,256]{0,1:T(8,128)} async-done(((f32[256,256]{0,1:T(8,128)}), f32[256,256]{0,1:T(8,128)}) %all-reduce.6.cloned.1.call-update) | async-done | bytes 262160 | tf_op jit(solution)/shard_map/psum | solution.py:73
  616.7 11.7 %cholesky.164 = f32[128,128]{1,0:T(8,128)S(1)} custom-call(f32[128,128]{1,0:T(8,128)S(1)} %cholesky.197), custom_call_target="Cholesky" | custom-call | tf_op jit(solution)/shard_map/jit(cholesky)/cholesky | solution.py:10
  628.5 9.8 %custom-call.20 = f32[1,128,128]{1,2,0:T(8,128)S(1)} custom-call(f32[1,128,128]{2,1,0:T(8,128)S(1)} %get-tuple-element.207), custom_call_target="InvertDiagBlocksLowerTriangular" | custom-call | tf_op jit(solution)/shard_map/jit(cholesky)/cholesky | solution.py:10
  638.7 11.7 %cholesky.181 = f32[128,128]{1,0:T(8,128)S(1)} custom-call(f32[128,128]{1,0:T(8,128)S(1)} %convolution_subtract_fusion.2), custom_call_target="Cholesky" | custom-call | tf_op jit(solution)/shard_map/jit(cholesky)/cholesky | solution.py:10
  653.1 4.1 while.31
  657.3 19.7 %custom-call.21 = f32[2,128,128]{1,2,0:T(8,128)S(1)} custom-call(f32[2,128,128]{2,1,0:T(8,128)S(1)} %get-tuple-element.133), custom_call_target="InvertDiagBlocksLowerTriangular" | custom-call | tf_op jit(solution)/shard_map/triangular_solve/custom-call.0 | solution.py:11
  (279 shorter events, 154.6 us)
Async XLA Ops:
  8.0 54.6 %all-gather.2.cloned.1.call-start = ((), (), s32[]{:S(2)}) async-start(), calls=%async_computation.3 | async-start | bytes 2162688 | tf_op jit(solution)/shard_map/all_gather | solution.py:48
  8.7 263.9 %all-reduce.4.cloned.1.call-start = ((), (), s32[]{:S(2)}) async-start(), calls=%async_computation.2 | async-start | bytes 524288 | tf_op jit(solution)/shard_map/psum | solution.py:47
  10.7 323.2 %reduce-scatter.3.cloned.1.call-start = ((), (), s32[]{:S(2)}) async-start(), calls=%async_computation.4 | async-start | bytes 1179648 | tf_op jit(solution)/shard_map/reduce_scatter | solution.py:67
  10.7 15.7 %copy-start.2 = (s32[1,1,16]{2,1,0:T(1,128)S(1)}, s32[1,1,16]{2,1,0:T(1,128)}, u32[]{:S(2)}) copy-start(s32[1,1,16]{2,1,0:T(1,128)} %param.18) | copy-start | bytes 196
  10.7 51.9 %copy-start.1 = (bf16[1024,256]{1,0:T(8,128)(2,1)S(1)}, bf16[1024,256]{1,0:T(8,128)(2,1)}, u32[]{:S(2)}) copy-start(bf16[1024,256]{1,0:T(8,128)(2,1)} %param.22) | copy-start | bytes 1572868
  10.7 51.9 %copy-start.3 = (s32[1,1,16]{2,1,0:T(1,128)S(1)}, s32[1,1,16]{2,1,0:T(1,128)}, u32[]{:S(2)}) copy-start(s32[1,1,16]{2,1,0:T(1,128)} %param.17) | copy-start | bytes 196
  10.7 51.9 %copy-start.4 = (s32[1,1,16]{2,1,0:T(1,128)S(1)}, s32[1,1,16]{2,1,0:T(1,128)}, u32[]{:S(2)}) copy-start(s32[1,1,16]{2,1,0:T(1,128)} %param.19) | copy-start | bytes 196
  206.9 1.0 copy-start
  207.9 407.6 %all-reduce.6.cloned.1.call-start = ((), (), s32[]{:S(2)}) async-start(), calls=%async_computation.5 | async-start | bytes 524288 | tf_op jit(solution)/shard_map/psum | solution.py:73
  362.9 314.1 %reduce-scatter.5.cloned.1.call-start = ((), (), s32[]{:S(2)}) async-start(), calls=%async_computation.6 | async-start | bytes 4325376 | tf_op jit(solution)/shard_map/reduce_scatter | solution.py:92
Sparse Core Ops, SparseCore 0:
  11.4 51.1 all-gather.1
  208.0 42.8 reduce-scatter.2
  525.1 93.6 reduce-scatter.4
Sparse Core Ops, SparseCore 1:
  14.7 257.9 all-reduce.3
  363.0 252.5 all-reduce.5
where the time goes:
time: 694 us; the launch traced here: 688 us
  waiting for transfers between devices  191 us (28%)
  loops' own time  155 us (22%)
  other arithmetic  143 us (21%)
  local copies, waits for them, and re-layouts  121 us (17%)
  matrix products  34.1 us (5%)
  blocking collectives  24.6 us (4%)
  between operations  18.1 us (3%)
    psum x1, waiting for transfers between devices, local(): gram_a = lax.psum(column_gram(a_half), ('wide', 'narrow'))  89.8 us
    another operation x1, loops' own time, local(): lax.fori_loop(0, live_count, second_step, jnp.zeros((width_slots, tile_ro...  79.1 us
    another operation x1, loops' own time, local(): lax.fori_loop(0, live_count, first_step, jnp.zeros((narrow_count * TI_DEV...  75.7 us
    another operation x13, other arithmetic, right_solve(): chol_lower = jnp.linalg.cholesky(matrix)  68.6 us
    psum x1, waiting for transfers between devices, local(): gram_b = lax.psum(column_gram(factor_b), ('wide', 'narrow'))  64.7 us
    another operation x5, other arithmetic, right_solve(): lax.linalg.triangular_solve(chol_lower, target, left_side=False, lower=Tr...  39.4 us
    all_gather x1, waiting for transfers between devices, local(): gathered = lax.all_gather(factor_b, 'wide', axis=0, tiled=True)  36.2 us
    all_gather x1, blocking collectives, local(): a_rows = lax.all_gather(a_half, 'narrow', axis=0, tiled=True)  24.6 us
  transfers between devices with their start and end apart: 5, of which 3 were waited for; matrix products, arithmetic and copies ran while one was open for 42% of the time, Pallas kernels for 0%

commit v1 on v0

--- a/solution.py
+++ b/solution.py
@@ -44,7 +44,7 @@
     owners = second_ids // second_local
     inside = second_ids % second_local
     gram_c = column_gram(factor_c)
-    gram_b = lax.psum(column_gram(factor_b), ("wide", "narrow"))
+    gram_b = lax.psum(lax.psum(column_gram(factor_b), "narrow"), "wide")
     gathered = lax.all_gather(factor_b, "wide", axis=0, tiled=True)
     b_tiles = gathered.reshape(wide_count * second_local, tile_rows, rank_width)
     b_pick = owners * second_local + inside

time: 694 us -> 660 us (0.951)
  waiting for transfers between devices: 191 us -> 158 us
    all_gather x1, waiting for transfers between devices: 36.2 us -> 0.03 us  [local(): gathered = lax.all_gather(factor_b, 'wide', axis=0, tiled=True)]
    psum x1, waiting for transfers between devices: 89.8 us -> 96.9 us  [local(): gram_a = lax.psum(column_gram(a_half), ('wide', 'narrow'))]
    psum x1 -> x2, waiting for transfers between devices: 64.7 us -> 60.9 us  [local(): gram_b = lax.psum(lax.psum(column_gram(factor_b), 'narrow'), 'wide')]
  transfers between devices with their start and end apart: 5 -> 6, of which waited for: 3 -> 2; matrix products, arithmetic and copies ran while one was open for 42% -> 44% of each run, Pallas kernels for 0% -> 0%
where the time goes in v1:
time: 660 us; the launch traced here: 654 us
  waiting for transfers between devices  158 us (24%)
  loops' own time  155 us (23%)
  other arithmetic  143 us (22%)
  local copies, waits for them, and re-layouts  121 us (18%)
  matrix products  34.1 us (5%)
  blocking collectives  23.1 us (4%)
  between operations  18.4 us (3%)
    psum x1, waiting for transfers between devices, local(): gram_a = lax.psum(column_gram(a_half), ('wide', 'narrow'))  96.9 us
    another operation x1, loops' own time, local(): lax.fori_loop(0, live_count, second_step, jnp.zeros((width_slots, tile_ro...  79.1 us
    another operation x1, loops' own time, local(): lax.fori_loop(0, live_count, first_step, jnp.zeros((narrow_count * TI_DEV...  75.7 us
    another operation x13, other arithmetic, right_solve(): chol_lower = jnp.linalg.cholesky(matrix)  68.6 us
    psum x2, waiting for transfers between devices, local(): gram_b = lax.psum(lax.psum(column_gram(factor_b), 'narrow'), 'wide')  60.9 us
    another operation x5, other arithmetic, right_solve(): lax.linalg.triangular_solve(chol_lower, target, left_side=False, lower=Tr...  39.4 us
    all_gather x1, blocking collectives, local(): a_rows = lax.all_gather(a_half, 'narrow', axis=0, tiled=True)  23.1 us
    dot_general x30, matrix products, depth_mix(): lax.dot_general(one_block, depth_rows, (((0,), (0,)), ((), ())), preferre...  22.6 us
  transfers between devices with their start and end apart: 6, of which 2 were waited for; matrix products, arithmetic and copies ran while one was open for 44% of the time, Pallas kernels for 0%

profile of v1, /device:TPU:2, one launch (start us, length us, event | category | flops | bytes accessed | tf_op | source)
XLA Modules:
  0.0 654.0 jit_solution(4381922706876876882)
XLA Ops:
  8.0 1.8 fusion.35
  10.6 15.6 %copy.22 = bf16[1,1,16,64,4096]{3,4,2,1,0:T(8,128)(2,1)} copy(bf16[1,1,16,64,4096]{4,3,2,1,0:T(8,128)(2,1)} %param.16) | data formatting | bytes 16777216 | tf_op args[0]
  26.2 60.8 %all-reduce.5.cloned.1.call-done = f32[256,256]{0,1:T(8,128)} async-done(((f32[256,256]{0,1:T(8,128)}), f32[256,256]{0,1:T(8,128)}) %all-reduce.5.cloned.1.call-update) | async-done | bytes 262160 | tf_op jit(solution)/shard_map/psum | solution.py:47
  87.3 144.1 %while.28 = (s32[]{:T(128)}, f32[16,64,256]{2,1,0:T(8,128)S(1)}, s32[]{:T(128)}, s32[16]{0:T(128)S(1)}, bf16[16,64,4096]{1,2,0:T(8,128)(2,1)}, /*index=5*/s32[16...) while((s32[]{:T(128)}, f32[16,64,256]{2,1,0:T(8,128)S(1)}, ...), condition=%wide.region_8.10_spmd, body=%wide.region_6.9_spmd.sunk | while | flops 136331280 | bytes 2556253 | solution.py:61
  234.0 11.7 %cholesky.130 = f32[128,128]{1,0:T(8,128)S(1)} custom-call(f32[128,128]{1,0:T(8,128)S(1)} %cholesky.194), custom_call_target="Cholesky" | custom-call | tf_op jit(solution)/shard_map/jit(cholesky)/cholesky | solution.py:10
  245.8 9.8 %custom-call.17 = f32[1,128,128]{1,2,0:T(8,128)S(1)} custom-call(f32[1,128,128]{2,1,0:T(8,128)S(1)} %get-tuple-element.211), custom_call_target="InvertDiagBlocksLowerTriangular" | custom-call | tf_op jit(solution)/shard_map/jit(cholesky)/cholesky | solution.py:10
  256.1 11.7 %cholesky.147 = f32[128,128]{1,0:T(8,128)S(1)} custom-call(f32[128,128]{1,0:T(8,128)S(1)} %convolution_subtract_fusion.5), custom_call_target="Cholesky" | custom-call | tf_op jit(solution)/shard_map/jit(cholesky)/cholesky | solution.py:10
  269.9 4.2 while.30
  274.1 19.7 %custom-call.18 = f32[2,128,128]{1,2,0:T(8,128)S(1)} custom-call(f32[2,128,128]{2,1,0:T(8,128)S(1)} %get-tuple-element.131), custom_call_target="InvertDiagBlocksLowerTriangular" | custom-call | tf_op jit(solution)/shard_map/triangular_solve/custom-call.0 | solution.py:11
  297.1 23.1 %all_gather.7 = bf16[1024,256]{0,1:T(8,128)(2,1)S(1)} all-gather(bf16[128,256]{0,1:T(8,128)(2,1)S(1)} %fusion.31), channel_id=1, replica_groups=mesh['wide'=32,'narrow'=8] {'narrow'}, dimensions={0}, use_global_device_ids=true | all-gather | bytes 589824 | tf_op jit(solution)/shard_map/all_gather | solution.py:72
  321.3 2.4 broadcast_in_dim.14
  323.8 159.6 %while.29 = (s32[]{:T(128)}, f32[64,64,256]{2,1,0:T(8,128)}, s32[]{:T(128)}, s32[16]{0:T(128)S(1)}, bf16[16,64,4096]{1,2,0:T(8,128)(2,1)}, /*index=5*/s32[16]{0:...) while((s32[]{:T(128)}, f32[64,64,256]{2,1,0:T(8,128)}, ...), condition=%wide.region_13.17_spmd, body=%wide.region_11.16_spmd.sunk | while | flops 136331280 | bytes 2556253 | solution.py:89
  332.9 1.5 fusion.72
  343.5 1.5 fusion.72
  354.1 1.5 fusion.72
  364.7 1.5 fusion.72
  375.3 1.5 fusion.72
  385.9 1.5 fusion.72
  407.1 1.5 fusion.72
  417.6 1.5 fusion.72
  428.2 1.5 fusion.72
  438.8 1.5 fusion.72
  449.4 1.5 fusion.72
  460.1 1.5 fusion.72
  470.7 1.5 fusion.72
  481.2 1.5 fusion.72
  484.2 96.9 %all-reduce.9.cloned.1.call-done = f32[256,256]{0,1:T(8,128)} async-done(((f32[256,256]{0,1:T(8,128)}), f32[256,256]{0,1:T(8,128)}) %all-reduce.9.cloned.1.call-update) | async-done | bytes 262160 | tf_op jit(solution)/shard_map/psum | solution.py:73
  582.3 11.7 %cholesky.164 = f32[128,128]{1,0:T(8,128)S(1)} custom-call(f32[128,128]{1,0:T(8,128)S(1)} %cholesky.197), custom_call_target="Cholesky" | custom-call | tf_op jit(solution)/shard_map/jit(cholesky)/cholesky | solution.py:10
  594.0 9.8 %custom-call.20 = f32[1,128,128]{1,2,0:T(8,128)S(1)} custom-call(f32[1,128,128]{2,1,0:T(8,128)S(1)} %get-tuple-element.207), custom_call_target="InvertDiagBlocksLowerTriangular" | custom-call | tf_op jit(solution)/shard_map/jit(cholesky)/cholesky | solution.py:10
  604.3 11.7 %cholesky.181 = f32[128,128]{1,0:T(8,128)S(1)} custom-call(f32[128,128]{1,0:T(8,128)S(1)} %convolution_subtract_fusion.2), custom_call_target="Cholesky" | custom-call | tf_op jit(solution)/shard_map/jit(cholesky)/cholesky | solution.py:10
  618.7 4.1 while.31
  622.9 19.7 %custom-call.21 = f32[2,128,128]{1,2,0:T(8,128)S(1)} custom-call(f32[2,128,128]{2,1,0:T(8,128)S(1)} %get-tuple-element.133), custom_call_target="InvertDiagBlocksLowerTriangular" | custom-call | tf_op jit(solution)/shard_map/triangular_solve/custom-call.0 | solution.py:11
  (282 shorter events, 153.0 us)
Async XLA Ops:
  8.0 79.1 %all-reduce.5.cloned.1.call-start = ((), (), s32[]{:S(2)}) async-start(), calls=%async_computation.2 | async-start | bytes 524288 | tf_op jit(solution)/shard_map/psum | solution.py:47
  9.9 77.3 %all-gather.2.cloned.1.call-start = ((), (), s32[]{:S(2)}) async-start(), calls=%async_computation.4 | async-start | bytes 2162688 | tf_op jit(solution)/shard_map/all_gather | solution.py:48
  10.5 222.0 %all-reduce.7.cloned.1.call-start = ((), (), s32[]{:S(2)}) async-start(), calls=%async_computation.3 | async-start | bytes 524288 | tf_op jit(solution)/shard_map/psum | solution.py:47
  10.5 15.7 %copy-start.2 = (s32[1,1,16]{2,1,0:T(1,128)S(1)}, s32[1,1,16]{2,1,0:T(1,128)}, u32[]{:S(2)}) copy-start(s32[1,1,16]{2,1,0:T(1,128)} %param.18) | copy-start | bytes 196
  10.6 76.7 %copy-start.1 = (bf16[1024,256]{1,0:T(8,128)(2,1)S(1)}, bf16[1024,256]{1,0:T(8,128)(2,1)}, u32[]{:S(2)}) copy-start(bf16[1024,256]{1,0:T(8,128)(2,1)} %param.22) | copy-start | bytes 1572868
  10.6 76.7 %copy-start.3 = (s32[1,1,16]{2,1,0:T(1,128)S(1)}, s32[1,1,16]{2,1,0:T(1,128)}, u32[]{:S(2)}) copy-start(s32[1,1,16]{2,1,0:T(1,128)} %param.17) | copy-start | bytes 196
  10.6 76.7 %copy-start.4 = (s32[1,1,16]{2,1,0:T(1,128)S(1)}, s32[1,1,16]{2,1,0:T(1,128)}, u32[]{:S(2)}) copy-start(s32[1,1,16]{2,1,0:T(1,128)} %param.19) | copy-start | bytes 196
  87.1 206.7 %reduce-scatter.3.cloned.1.call-start = ((), (), s32[]{:S(2)}) async-start(), calls=%async_computation.5 | async-start | bytes 1179648 | tf_op jit(solution)/shard_map/reduce_scatter | solution.py:67
  231.4 1.0 copy-start
  232.4 348.6 %all-reduce.9.cloned.1.call-start = ((), (), s32[]{:S(2)}) async-start(), calls=%async_computation.6 | async-start | bytes 524288 | tf_op jit(solution)/shard_map/psum | solution.py:73
  321.3 321.3 %reduce-scatter.5.cloned.1.call-start = ((), (), s32[]{:S(2)}) async-start(), calls=%async_computation.7 | async-start | bytes 4325376 | tf_op jit(solution)/shard_map/reduce_scatter | solution.py:92
Sparse Core Ops, SparseCore 0:
  11.1 75.9 all-reduce.4
  232.6 44.1 reduce-scatter.2
  321.4 259.6 all-reduce.8
Sparse Core Ops, SparseCore 1:
  12.9 51.1 all-gather.1
  87.2 110.0 all-reduce.6
  483.5 104.6 reduce-scatter.4
